TPU v7x, 768 devices: a whole 4x8x12 slice. The times are simulated.
768 devices in a mesh: orb: 12 (over x, z_lo), sx: 8 (over y), sy: 8 (over z_hi, core).
Axes of the slice: x: 4, y: 8, z: 12 (z_hi: 4, z_lo: 3; z = z_hi * 3 + z_lo), core: 2. Of those that a mesh axis runs over, the one named last changes fastest.
Arguments:
- orbitals: bfloat16 [64, 64, 24576], P('sx', 'sy', 'orb'), may hold values from -6 to 6
- src_owner: int32 [2, 2], replicated, may hold values from 0 to 11
- src_slot: int32 [2, 2], replicated, may hold values from 0 to 63
Outputs:
- exchange_field: float32 [64, 64, 24576], P('sx', 'sy', 'orb')
All inputs are finite; a program needn't handle non-finite values.
Results may differ from a plain program's by a relative error of at most 0.0003.
Values may be sent and summed in bfloat16 or wider, within the bound.
A program may use at most 128 MiB of HBM per device.

v0:
```python
import jax
import jax.numpy as jnp
from jax import lax
from jax.sharding import PartitionSpec as P

NZ = 32
SRC = 2
ROUNDS = 2
DEGREE = 4


cheb_coeffs = (
    1.021021021021021,
    -1.7357357357357357,
    1.4753753753753753,
    -1.254069069069069,
    1.0659587087087088,
)


def extended(block, sides, width):
    for axis, dim in sides:
        count = lax.axis_size(axis)
        forward = [(i, i + 1) for i in range(count - 1)]
        forward.append((count - 1, 0))
        backward = [(target, source) for source, target in forward]
        low = lax.ppermute(
            lax.slice_in_dim(block, block.shape[dim] - width, None, axis=dim), axis, forward
        )
        high = lax.ppermute(lax.slice_in_dim(block, 0, width, axis=dim), axis, backward)
        block = jnp.concatenate([low, block, high], axis=dim)
    return block


def spread_2(block, axis, owner):
    block = jnp.where(lax.axis_index(axis) == owner, block, jnp.zeros_like(block))
    return lax.psum(block, axis)


def crop(field, margin):
    return field[margin : field.shape[0] - margin, margin : field.shape[1] - margin]


def screened(padded):
    core = crop(padded, 1)
    side = padded[2:, 1:-1] + padded[:-2, 1:-1]
    side = side + padded[1:-1, 2:] + padded[1:-1, :-2]
    lane = lax.broadcasted_iota(jnp.int32, core.shape, 2) % NZ
    zeros = jnp.zeros(core.shape[:2] + (1,), core.dtype)
    upper = jnp.where(lane == NZ - 1, 0.0, jnp.concatenate([core[..., 1:], zeros], axis=2))
    lower = jnp.where(lane == 0, 0.0, jnp.concatenate([zeros, core[..., :-1]], axis=2))
    side = side + upper + lower
    return -side / 6.0


def widen_one(field):
    return extended(field, (("sx", 0), ("sy", 1)), 1)


def potential(density):
    t_prev = density
    t_cur = screened(widen_one(density))
    total = cheb_coeffs[0] * t_prev + cheb_coeffs[1] * t_cur
    for order in range(2, DEGREE + 1):
        t_next = 2.0 * screened(widen_one(t_cur)) - t_prev
        total = total + cheb_coeffs[order] * t_next
        t_prev, t_cur = (t_cur, t_next)
    return total


def own_block(orbitals, slot):
    rows_x, rows_y, _ = orbitals.shape
    block = lax.dynamic_slice_in_dim(orbitals, slot * NZ, NZ, 2)
    return block.reshape(rows_x, rows_y * NZ)


def fetch_single(orbitals, owner, slot):
    rows_x, rows_y, _ = orbitals.shape
    got = spread_2(own_block(orbitals, slot), "orb", owner)
    return got.reshape(rows_x, rows_y, NZ)


def fetch_sources(orbitals, src_owner, src_slot, rnd):
    return [
        fetch_single(orbitals, src_owner[rnd, place], src_slot[rnd, place]) for place in range(SRC)
    ]


def body(orbitals, src_owner, src_slot):
    rows_x, rows_y, width = orbitals.shape
    held = width // NZ
    exchange_field = jnp.zeros(orbitals.shape, jnp.float32)
    own = orbitals.astype(jnp.float32)
    for rnd in range(ROUNDS):
        sources = fetch_sources(orbitals, src_owner, src_slot, rnd)
        tiled = [jnp.tile(source.astype(jnp.float32), (1, 1, held)) for source in sources]
        density = jnp.concatenate([own * spread for spread in tiled], axis=2)
        total = potential(density)
        for place in range(SRC):
            exchange_field = (
                exchange_field - total[..., place * width : (place + 1) * width] * tiled[place]
            )
    return exchange_field


def solution(mesh):
    in_specs = (P("sx", "sy", "orb"), P(), P())
    out_specs = P("sx", "sy", "orb")
    return jax.shard_map(body, mesh=mesh, in_specs=in_specs, out_specs=out_specs, check_vma=False)
```

profile of v0, /device:TPU:1, one launch (start us, length us, event | category | flops | bytes accessed | tf_op | source)
XLA Modules:
  0.0 227.1 jit_solution(9487793500359119248)
XLA Ops:
  8.9 48.3 %all-reduce.16 = (bf16[8,8,32]{2,1,0:T(8,128)(2,1)S(1)}, bf16[8,8,32]{2,1,0:T(8,128)(2,1)S(1)}, bf16[8,8,32]{2,1,0:T(8,128)(2,1)S(1)}, bf16[8,8,32]{2,1,0:T(8,128)(2,1)S(1)}) all-reduce(bf16[8,8,32]{2,1,0:T(8,128)(2,1)S(1)} %get-tuple-element.67, ...), channel_id=1, replica_groups=mesh['orb'=12,'sx'=8,'sy'=8] {'orb'}, use_global_device_ids=true, to_apply=%region_0.1 | all-reduce | flops 8192 | bytes 32768 | tf_op jit(solution)/shard_map/psum | solution.py:37
  64.7 5.3 %collective-permute-start.16 = (f32[1,8,4096]{2,1,0:T(8,128)S(1)}, f32[1,8,4096]{2,1,0:T(8,128)S(1)}, u32[]{:S(2)}, u32[]{:S(2)}) collective-permute-start(f32[1,8,4096]{2,1,0:T(8,128)S(1)} %get-tuple-element.58), channel_id=1, source_target_pairs={{8,0},{16,8},{24,16},{32,24},{40,32},{48,40},{56,48},{0,56},{9,1},... | collective-permute-start | bytes 393224 | tf_op jit(solution)/shard_map/ppermute | solution.py:30
  70.0 1.9 collective-permute-start.17
  71.9 4.6 %collective-permute-start = (f32[1,8,4096]{2,1,0:T(8,128)S(1)}, f32[1,8,4096]{2,1,0:T(8,128)S(1)}, u32[]{:S(2)}, u32[]{:S(2)}) collective-permute-start(f32[1,8,4096]{2,1,0:T(8,128)S(1)} %get-tuple-element.42), channel_id=1, source_target_pairs={{8,0},{16,8},{24,16},{32,24},{40,32},{48,40},{56,48},{0,56},{9,1},... | collective-permute-start | bytes 393224 | tf_op jit(solution)/shard_map/ppermute | solution.py:30
  76.5 1.9 collective-permute-start.1
  79.5 28.1 %collective-permute-start.19 = (f32[10,1,4096]{2,1,0:T(1,128)S(1)}, f32[10,1,4096]{2,1,0:T(1,128)S(1)}, u32[]{:S(2)}, u32[]{:S(2)}) collective-permute-start(f32[10,1,4096]{2,1,0:T(1,128)S(1)} %get-tuple-element.28), channel_id=1, source_target_pairs={{0,1},{1,2},{2,3},{3,4},{4,5},{5,6},{6,7},{7,0},{8,9},{9,10},{10,1... | collective-permute-start | bytes 491528 | tf_op jit(solution)/shard_map/ppermute | solution.py:27
  107.7 1.9 collective-permute-start.18
  109.9 5.4 %collective-permute-start.3 = (f32[10,1,4096]{2,1,0:T(1,128)S(1)}, f32[10,1,4096]{2,1,0:T(1,128)S(1)}, u32[]{:S(2)}, u32[]{:S(2)}) collective-permute-start(f32[10,1,4096]{2,1,0:T(1,128)S(1)} %get-tuple-element.20), channel_id=1, source_target_pairs={{0,1},{1,2},{2,3},{3,4},{4,5},{5,6},{6,7},{7,0},{8,9},{9,10},{10,1... | collective-permute-start | bytes 491528 | tf_op jit(solution)/shard_map/ppermute | solution.py:27
  115.3 1.9 collective-permute-start.2
  118.8 4.8 %collective-permute-start.20 = (f32[1,8,4096]{2,1,0:T(8,128)S(1)}, f32[1,8,4096]{2,1,0:T(8,128)S(1)}, u32[]{:S(2)}, u32[]{:S(2)}) collective-permute-start(f32[1,8,4096]{2,1,0:T(8,128)S(1)} %get-tuple-element.56), channel_id=1, source_target_pairs={{8,0},{16,8},{24,16},{32,24},{40,32},{48,40},{56,48},{0,56},{9,1},... | collective-permute-start | bytes 393224 | tf_op jit(solution)/shard_map/ppermute | solution.py:30
  123.6 1.9 collective-permute-start.21
  127.6 4.9 %collective-permute-start.4 = (f32[1,8,4096]{2,1,0:T(8,128)S(1)}, f32[1,8,4096]{2,1,0:T(8,128)S(1)}, u32[]{:S(2)}, u32[]{:S(2)}) collective-permute-start(f32[1,8,4096]{2,1,0:T(8,128)S(1)} %get-tuple-element.40), channel_id=1, source_target_pairs={{8,0},{16,8},{24,16},{32,24},{40,32},{48,40},{56,48},{0,56},{9,1},... | collective-permute-start | bytes 393224 | tf_op jit(solution)/shard_map/ppermute | solution.py:30
  132.5 1.9 collective-permute-start.5
  134.7 4.7 %collective-permute-start.23 = (f32[10,1,4096]{2,1,0:T(1,128)S(1)}, f32[10,1,4096]{2,1,0:T(1,128)S(1)}, u32[]{:S(2)}, u32[]{:S(2)}) collective-permute-start(f32[10,1,4096]{2,1,0:T(1,128)S(1)} %get-tuple-element.26), channel_id=1, source_target_pairs={{0,1},{1,2},{2,3},{3,4},{4,5},{5,6},{6,7},{7,0},{8,9},{9,10},{10,1... | collective-permute-start | bytes 491528 | tf_op jit(solution)/shard_map/ppermute | solution.py:27
  139.4 1.9 collective-permute-start.22
  141.7 5.4 %collective-permute-start.7 = (f32[10,1,4096]{2,1,0:T(1,128)S(1)}, f32[10,1,4096]{2,1,0:T(1,128)S(1)}, u32[]{:S(2)}, u32[]{:S(2)}) collective-permute-start(f32[10,1,4096]{2,1,0:T(1,128)S(1)} %get-tuple-element.18), channel_id=1, source_target_pairs={{0,1},{1,2},{2,3},{3,4},{4,5},{5,6},{6,7},{7,0},{8,9},{9,10},{10,1... | collective-permute-start | bytes 491528 | tf_op jit(solution)/shard_map/ppermute | solution.py:27
  147.1 1.9 collective-permute-start.6
  149.0 2.5 %collective-permute-done.22 = f32[10,1,4096]{2,1,0:T(1,128)S(1)} collective-permute-done((f32[10,1,4096]{2,1,0:T(1,128)S(1)}, f32[10,1,4096]{2,1,0:T(1,128)S(1)}, u32[]{:S(2)}, u32[]{:S(2)}) %collective-permute-start.22) | collective-permute-done | bytes 163872 | tf_op jit(solution)/shard_map/ppermute | solution.py:30
  152.7 4.8 %collective-permute-start.24 = (f32[1,8,4096]{2,1,0:T(8,128)S(1)}, f32[1,8,4096]{2,1,0:T(8,128)S(1)}, u32[]{:S(2)}, u32[]{:S(2)}) collective-permute-start(f32[1,8,4096]{2,1,0:T(8,128)S(1)} %get-tuple-element.52), channel_id=1, source_target_pairs={{8,0},{16,8},{24,16},{32,24},{40,32},{48,40},{56,48},{0,56},{9,1},... | collective-permute-start | bytes 393224 | tf_op jit(solution)/shard_map/ppermute | solution.py:30
  157.6 2.1 collective-permute-start.25
  160.8 4.6 %collective-permute-start.8 = (f32[1,8,4096]{2,1,0:T(8,128)S(1)}, f32[1,8,4096]{2,1,0:T(8,128)S(1)}, u32[]{:S(2)}, u32[]{:S(2)}) collective-permute-start(f32[1,8,4096]{2,1,0:T(8,128)S(1)} %get-tuple-element.36), channel_id=1, source_target_pairs={{8,0},{16,8},{24,16},{32,24},{40,32},{48,40},{56,48},{0,56},{9,1},... | collective-permute-start | bytes 393224 | tf_op jit(solution)/shard_map/ppermute | solution.py:30
  167.6 3.9 %collective-permute-start.27 = (f32[10,1,4096]{2,1,0:T(1,128)S(1)}, f32[10,1,4096]{2,1,0:T(1,128)S(1)}, u32[]{:S(2)}, u32[]{:S(2)}) collective-permute-start(f32[10,1,4096]{2,1,0:T(1,128)S(1)} %get-tuple-element.24), channel_id=1, source_target_pairs={{0,1},{1,2},{2,3},{3,4},{4,5},{5,6},{6,7},{7,0},{8,9},{9,10},{10,1... | collective-permute-start | bytes 491528 | tf_op jit(solution)/shard_map/ppermute | solution.py:27
  173.8 6.2 %collective-permute-start.11 = (f32[10,1,4096]{2,1,0:T(1,128)S(1)}, f32[10,1,4096]{2,1,0:T(1,128)S(1)}, u32[]{:S(2)}, u32[]{:S(2)}) collective-permute-start(f32[10,1,4096]{2,1,0:T(1,128)S(1)} %get-tuple-element.16), channel_id=1, source_target_pairs={{0,1},{1,2},{2,3},{3,4},{4,5},{5,6},{6,7},{7,0},{8,9},{9,10},{10,1... | collective-permute-start | bytes 491528 | tf_op jit(solution)/shard_map/ppermute | solution.py:27
  180.0 1.9 collective-permute-start.10
  181.9 2.6 %collective-permute-done.26 = f32[10,1,4096]{2,1,0:T(1,128)S(1)} collective-permute-done((f32[10,1,4096]{2,1,0:T(1,128)S(1)}, f32[10,1,4096]{2,1,0:T(1,128)S(1)}, u32[]{:S(2)}, u32[]{:S(2)}) %collective-permute-start.26) | collective-permute-done | bytes 163872 | tf_op jit(solution)/shard_map/ppermute | solution.py:30
  185.7 2.0 collective-permute-start.28
  187.7 3.3 %collective-permute-start.29 = (f32[1,8,4096]{2,1,0:T(8,128)S(1)}, f32[1,8,4096]{2,1,0:T(8,128)S(1)}, u32[]{:S(2)}, u32[]{:S(2)}) collective-permute-start(f32[1,8,4096]{2,1,0:T(8,128)S(1)} %get-tuple-element.47), channel_id=1, source_target_pairs={{0,8},{8,16},{16,24},{24,32},{32,40},{40,48},{48,56},{56,0},{1,9},... | collective-permute-start | bytes 393224 | tf_op jit(solution)/shard_map/ppermute | solution.py:27
  192.2 4.0 %collective-permute-start.12 = (f32[1,8,4096]{2,1,0:T(8,128)S(1)}, f32[1,8,4096]{2,1,0:T(8,128)S(1)}, u32[]{:S(2)}, u32[]{:S(2)}) collective-permute-start(f32[1,8,4096]{2,1,0:T(8,128)S(1)} %get-tuple-element.32), channel_id=1, source_target_pairs={{8,0},{16,8},{24,16},{32,24},{40,32},{48,40},{56,48},{0,56},{9,1},... | collective-permute-start | bytes 393224 | tf_op jit(solution)/shard_map/ppermute | solution.py:30
  198.4 7.4 %collective-permute-start.31 = (f32[10,1,4096]{2,1,0:T(1,128)S(1)}, f32[10,1,4096]{2,1,0:T(1,128)S(1)}, u32[]{:S(2)}, u32[]{:S(2)}) collective-permute-start(f32[10,1,4096]{2,1,0:T(1,128)S(1)} %get-tuple-element.22), channel_id=1, source_target_pairs={{0,1},{1,2},{2,3},{3,4},{4,5},{5,6},{6,7},{7,0},{8,9},{9,10},{10,1... | collective-permute-start | bytes 491528 | tf_op jit(solution)/shard_map/ppermute | solution.py:27
  208.1 5.8 %collective-permute-start.15 = (f32[10,1,4096]{2,1,0:T(1,128)S(1)}, f32[10,1,4096]{2,1,0:T(1,128)S(1)}, u32[]{:S(2)}, u32[]{:S(2)}) collective-permute-start(f32[10,1,4096]{2,1,0:T(1,128)S(1)} %get-tuple-element.14), channel_id=1, source_target_pairs={{0,1},{1,2},{2,3},{3,4},{4,5},{5,6},{6,7},{7,0},{8,9},{9,10},{10,1... | collective-permute-start | bytes 491528 | tf_op jit(solution)/shard_map/ppermute | solution.py:27
  213.9 1.9 collective-permute-start.14
  217.4 7.1 %collective-permute-done.14 = f32[10,1,4096]{2,1,0:T(1,128)S(1)} collective-permute-done((f32[10,1,4096]{2,1,0:T(1,128)S(1)}, f32[10,1,4096]{2,1,0:T(1,128)S(1)}, u32[]{:S(2)}, u32[]{:S(2)}) %collective-permute-start.14) | collective-permute-done | bytes 163872 | tf_op jit(solution)/shard_map/ppermute | solution.py:30
  (86 shorter events, 34.1 us)
Async XLA Ops:
  64.7 14.6 %collective-permute-start.16 = (f32[1,8,4096]{2,1,0:T(8,128)S(1)}, f32[1,8,4096]{2,1,0:T(8,128)S(1)}, u32[]{:S(2)}, u32[]{:S(2)}) collective-permute-start(f32[1,8,4096]{2,1,0:T(8,128)S(1)} %get-tuple-element.58), channel_id=1, source_target_pairs={{8,0},{16,8},{24,16},{32,24},{40,32},{48,40},{56,48},{0,56},{9,1},... | collective-permute-start | bytes 393224 | tf_op jit(solution)/shard_map/ppermute | solution.py:30
  70.0 9.3 %collective-permute-start.17 = (f32[1,8,4096]{2,1,0:T(8,128)S(1)}, f32[1,8,4096]{2,1,0:T(8,128)S(1)}, u32[]{:S(2)}, u32[]{:S(2)}) collective-permute-start(f32[1,8,4096]{2,1,0:T(8,128)S(1)} %get-tuple-element.57), channel_id=1, source_target_pairs={{0,8},{8,16},{16,24},{24,32},{32,40},{40,48},{48,56},{56,0},{1,9},... | collective-permute-start | bytes 393224 | tf_op jit(solution)/shard_map/ppermute | solution.py:27
  71.9 37.7 %collective-permute-start = (f32[1,8,4096]{2,1,0:T(8,128)S(1)}, f32[1,8,4096]{2,1,0:T(8,128)S(1)}, u32[]{:S(2)}, u32[]{:S(2)}) collective-permute-start(f32[1,8,4096]{2,1,0:T(8,128)S(1)} %get-tuple-element.42), channel_id=1, source_target_pairs={{8,0},{16,8},{24,16},{32,24},{40,32},{48,40},{56,48},{0,56},{9,1},... | collective-permute-start | bytes 393224 | tf_op jit(solution)/shard_map/ppermute | solution.py:30
  76.5 33.1 %collective-permute-start.1 = (f32[1,8,4096]{2,1,0:T(8,128)S(1)}, f32[1,8,4096]{2,1,0:T(8,128)S(1)}, u32[]{:S(2)}, u32[]{:S(2)}) collective-permute-start(f32[1,8,4096]{2,1,0:T(8,128)S(1)} %get-tuple-element.41), channel_id=1, source_target_pairs={{0,8},{8,16},{16,24},{24,32},{32,40},{40,48},{48,56},{56,0},{1,9},... | collective-permute-start | bytes 393224 | tf_op jit(solution)/shard_map/ppermute | solution.py:27
  79.5 37.7 %collective-permute-start.19 = (f32[10,1,4096]{2,1,0:T(1,128)S(1)}, f32[10,1,4096]{2,1,0:T(1,128)S(1)}, u32[]{:S(2)}, u32[]{:S(2)}) collective-permute-start(f32[10,1,4096]{2,1,0:T(1,128)S(1)} %get-tuple-element.28), channel_id=1, source_target_pairs={{0,1},{1,2},{2,3},{3,4},{4,5},{5,6},{6,7},{7,0},{8,9},{9,10},{10,1... | collective-permute-start | bytes 491528 | tf_op jit(solution)/shard_map/ppermute | solution.py:27
  107.7 10.0 %collective-permute-start.18 = (f32[10,1,4096]{2,1,0:T(1,128)S(1)}, f32[10,1,4096]{2,1,0:T(1,128)S(1)}, u32[]{:S(2)}, u32[]{:S(2)}) collective-permute-start(f32[10,1,4096]{2,1,0:T(1,128)S(1)} %get-tuple-element.27), channel_id=1, source_target_pairs={{1,0},{2,1},{3,2},{4,3},{5,4},{6,5},{7,6},{0,7},{9,8},{10,9},{11,1... | collective-permute-start | bytes 491528 | tf_op jit(solution)/shard_map/ppermute | solution.py:30
  109.9 15.7 %collective-permute-start.3 = (f32[10,1,4096]{2,1,0:T(1,128)S(1)}, f32[10,1,4096]{2,1,0:T(1,128)S(1)}, u32[]{:S(2)}, u32[]{:S(2)}) collective-permute-start(f32[10,1,4096]{2,1,0:T(1,128)S(1)} %get-tuple-element.20), channel_id=1, source_target_pairs={{0,1},{1,2},{2,3},{3,4},{4,5},{5,6},{6,7},{7,0},{8,9},{9,10},{10,1... | collective-permute-start | bytes 491528 | tf_op jit(solution)/shard_map/ppermute | solution.py:27
  115.3 11.2 %collective-permute-start.2 = (f32[10,1,4096]{2,1,0:T(1,128)S(1)}, f32[10,1,4096]{2,1,0:T(1,128)S(1)}, u32[]{:S(2)}, u32[]{:S(2)}) collective-permute-start(f32[10,1,4096]{2,1,0:T(1,128)S(1)} %get-tuple-element.19), channel_id=1, source_target_pairs={{1,0},{2,1},{3,2},{4,3},{5,4},{6,5},{7,6},{0,7},{9,8},{10,9},{11,1... | collective-permute-start | bytes 491528 | tf_op jit(solution)/shard_map/ppermute | solution.py:30
  118.8 15.6 %collective-permute-start.20 = (f32[1,8,4096]{2,1,0:T(8,128)S(1)}, f32[1,8,4096]{2,1,0:T(8,128)S(1)}, u32[]{:S(2)}, u32[]{:S(2)}) collective-permute-start(f32[1,8,4096]{2,1,0:T(8,128)S(1)} %get-tuple-element.56), channel_id=1, source_target_pairs={{8,0},{16,8},{24,16},{32,24},{40,32},{48,40},{56,48},{0,56},{9,1},... | collective-permute-start | bytes 393224 | tf_op jit(solution)/shard_map/ppermute | solution.py:30
  123.6 10.8 %collective-permute-start.21 = (f32[1,8,4096]{2,1,0:T(8,128)S(1)}, f32[1,8,4096]{2,1,0:T(8,128)S(1)}, u32[]{:S(2)}, u32[]{:S(2)}) collective-permute-start(f32[1,8,4096]{2,1,0:T(8,128)S(1)} %get-tuple-element.55), channel_id=1, source_target_pairs={{0,8},{8,16},{16,24},{24,32},{32,40},{40,48},{48,56},{56,0},{1,9},... | collective-permute-start | bytes 393224 | tf_op jit(solution)/shard_map/ppermute | solution.py:27
  127.6 13.7 %collective-permute-start.4 = (f32[1,8,4096]{2,1,0:T(8,128)S(1)}, f32[1,8,4096]{2,1,0:T(8,128)S(1)}, u32[]{:S(2)}, u32[]{:S(2)}) collective-permute-start(f32[1,8,4096]{2,1,0:T(8,128)S(1)} %get-tuple-element.40), channel_id=1, source_target_pairs={{8,0},{16,8},{24,16},{32,24},{40,32},{48,40},{56,48},{0,56},{9,1},... | collective-permute-start | bytes 393224 | tf_op jit(solution)/shard_map/ppermute | solution.py:30
  132.5 8.9 %collective-permute-start.5 = (f32[1,8,4096]{2,1,0:T(8,128)S(1)}, f32[1,8,4096]{2,1,0:T(8,128)S(1)}, u32[]{:S(2)}, u32[]{:S(2)}) collective-permute-start(f32[1,8,4096]{2,1,0:T(8,128)S(1)} %get-tuple-element.39), channel_id=1, source_target_pairs={{0,8},{8,16},{16,24},{24,32},{32,40},{40,48},{48,56},{56,0},{1,9},... | collective-permute-start | bytes 393224 | tf_op jit(solution)/shard_map/ppermute | solution.py:27
  134.7 14.3 %collective-permute-start.23 = (f32[10,1,4096]{2,1,0:T(1,128)S(1)}, f32[10,1,4096]{2,1,0:T(1,128)S(1)}, u32[]{:S(2)}, u32[]{:S(2)}) collective-permute-start(f32[10,1,4096]{2,1,0:T(1,128)S(1)} %get-tuple-element.26), channel_id=1, source_target_pairs={{0,1},{1,2},{2,3},{3,4},{4,5},{5,6},{6,7},{7,0},{8,9},{9,10},{10,1... | collective-permute-start | bytes 491528 | tf_op jit(solution)/shard_map/ppermute | solution.py:27
  139.4 12.1 %collective-permute-start.22 = (f32[10,1,4096]{2,1,0:T(1,128)S(1)}, f32[10,1,4096]{2,1,0:T(1,128)S(1)}, u32[]{:S(2)}, u32[]{:S(2)}) collective-permute-start(f32[10,1,4096]{2,1,0:T(1,128)S(1)} %get-tuple-element.25), channel_id=1, source_target_pairs={{1,0},{2,1},{3,2},{4,3},{5,4},{6,5},{7,6},{0,7},{9,8},{10,9},{11,1... | collective-permute-start | bytes 491528 | tf_op jit(solution)/shard_map/ppermute | solution.py:30
  141.7 18.0 %collective-permute-start.7 = (f32[10,1,4096]{2,1,0:T(1,128)S(1)}, f32[10,1,4096]{2,1,0:T(1,128)S(1)}, u32[]{:S(2)}, u32[]{:S(2)}) collective-permute-start(f32[10,1,4096]{2,1,0:T(1,128)S(1)} %get-tuple-element.18), channel_id=1, source_target_pairs={{0,1},{1,2},{2,3},{3,4},{4,5},{5,6},{6,7},{7,0},{8,9},{9,10},{10,1... | collective-permute-start | bytes 491528 | tf_op jit(solution)/shard_map/ppermute | solution.py:27
  147.1 12.6 %collective-permute-start.6 = (f32[10,1,4096]{2,1,0:T(1,128)S(1)}, f32[10,1,4096]{2,1,0:T(1,128)S(1)}, u32[]{:S(2)}, u32[]{:S(2)}) collective-permute-start(f32[10,1,4096]{2,1,0:T(1,128)S(1)} %get-tuple-element.17), channel_id=1, source_target_pairs={{1,0},{2,1},{3,2},{4,3},{5,4},{6,5},{7,6},{0,7},{9,8},{10,9},{11,1... | collective-permute-start | bytes 491528 | tf_op jit(solution)/shard_map/ppermute | solution.py:30
  152.7 14.6 %collective-permute-start.24 = (f32[1,8,4096]{2,1,0:T(8,128)S(1)}, f32[1,8,4096]{2,1,0:T(8,128)S(1)}, u32[]{:S(2)}, u32[]{:S(2)}) collective-permute-start(f32[1,8,4096]{2,1,0:T(8,128)S(1)} %get-tuple-element.52), channel_id=1, source_target_pairs={{8,0},{16,8},{24,16},{32,24},{40,32},{48,40},{56,48},{0,56},{9,1},... | collective-permute-start | bytes 393224 | tf_op jit(solution)/shard_map/ppermute | solution.py:30
  157.6 9.8 %collective-permute-start.25 = (f32[1,8,4096]{2,1,0:T(8,128)S(1)}, f32[1,8,4096]{2,1,0:T(8,128)S(1)}, u32[]{:S(2)}, u32[]{:S(2)}) collective-permute-start(f32[1,8,4096]{2,1,0:T(8,128)S(1)} %get-tuple-element.51), channel_id=1, source_target_pairs={{0,8},{8,16},{16,24},{24,32},{32,40},{40,48},{48,56},{56,0},{1,9},... | collective-permute-start | bytes 393224 | tf_op jit(solution)/shard_map/ppermute | solution.py:27
  160.8 12.7 %collective-permute-start.8 = (f32[1,8,4096]{2,1,0:T(8,128)S(1)}, f32[1,8,4096]{2,1,0:T(8,128)S(1)}, u32[]{:S(2)}, u32[]{:S(2)}) collective-permute-start(f32[1,8,4096]{2,1,0:T(8,128)S(1)} %get-tuple-element.36), channel_id=1, source_target_pairs={{8,0},{16,8},{24,16},{32,24},{40,32},{48,40},{56,48},{0,56},{9,1},... | collective-permute-start | bytes 393224 | tf_op jit(solution)/shard_map/ppermute | solution.py:30
  165.4 8.1 %collective-permute-start.9 = (f32[1,8,4096]{2,1,0:T(8,128)S(1)}, f32[1,8,4096]{2,1,0:T(8,128)S(1)}, u32[]{:S(2)}, u32[]{:S(2)}) collective-permute-start(f32[1,8,4096]{2,1,0:T(8,128)S(1)} %get-tuple-element.35), channel_id=1, source_target_pairs={{0,8},{8,16},{16,24},{24,32},{32,40},{40,48},{48,56},{56,0},{1,9},... | collective-permute-start | bytes 393224 | tf_op jit(solution)/shard_map/ppermute | solution.py:27
  167.6 14.3 %collective-permute-start.27 = (f32[10,1,4096]{2,1,0:T(1,128)S(1)}, f32[10,1,4096]{2,1,0:T(1,128)S(1)}, u32[]{:S(2)}, u32[]{:S(2)}) collective-permute-start(f32[10,1,4096]{2,1,0:T(1,128)S(1)} %get-tuple-element.24), channel_id=1, source_target_pairs={{0,1},{1,2},{2,3},{3,4},{4,5},{5,6},{6,7},{7,0},{8,9},{9,10},{10,1... | collective-permute-start | bytes 491528 | tf_op jit(solution)/shard_map/ppermute | solution.py:27
  171.6 13.0 %collective-permute-start.26 = (f32[10,1,4096]{2,1,0:T(1,128)S(1)}, f32[10,1,4096]{2,1,0:T(1,128)S(1)}, u32[]{:S(2)}, u32[]{:S(2)}) collective-permute-start(f32[10,1,4096]{2,1,0:T(1,128)S(1)} %get-tuple-element.23), channel_id=1, source_target_pairs={{1,0},{2,1},{3,2},{4,3},{5,4},{6,5},{7,6},{0,7},{9,8},{10,9},{11,1... | collective-permute-start | bytes 491528 | tf_op jit(solution)/shard_map/ppermute | solution.py:30
  173.8 17.2 %collective-permute-start.11 = (f32[10,1,4096]{2,1,0:T(1,128)S(1)}, f32[10,1,4096]{2,1,0:T(1,128)S(1)}, u32[]{:S(2)}, u32[]{:S(2)}) collective-permute-start(f32[10,1,4096]{2,1,0:T(1,128)S(1)} %get-tuple-element.16), channel_id=1, source_target_pairs={{0,1},{1,2},{2,3},{3,4},{4,5},{5,6},{6,7},{7,0},{8,9},{9,10},{10,1... | collective-permute-start | bytes 491528 | tf_op jit(solution)/shard_map/ppermute | solution.py:27
  180.0 11.1 %collective-permute-start.10 = (f32[10,1,4096]{2,1,0:T(1,128)S(1)}, f32[10,1,4096]{2,1,0:T(1,128)S(1)}, u32[]{:S(2)}, u32[]{:S(2)}) collective-permute-start(f32[10,1,4096]{2,1,0:T(1,128)S(1)} %get-tuple-element.15), channel_id=1, source_target_pairs={{1,0},{2,1},{3,2},{4,3},{5,4},{6,5},{7,6},{0,7},{9,8},{10,9},{11,1... | collective-permute-start | bytes 491528 | tf_op jit(solution)/shard_map/ppermute | solution.py:30
  185.7 12.4 %collective-permute-start.28 = (f32[1,8,4096]{2,1,0:T(8,128)S(1)}, f32[1,8,4096]{2,1,0:T(8,128)S(1)}, u32[]{:S(2)}, u32[]{:S(2)}) collective-permute-start(f32[1,8,4096]{2,1,0:T(8,128)S(1)} %get-tuple-element.48), channel_id=1, source_target_pairs={{8,0},{16,8},{24,16},{32,24},{40,32},{48,40},{56,48},{0,56},{9,1},... | collective-permute-start | bytes 393224 | tf_op jit(solution)/shard_map/ppermute | solution.py:30
  187.7 10.5 %collective-permute-start.29 = (f32[1,8,4096]{2,1,0:T(8,128)S(1)}, f32[1,8,4096]{2,1,0:T(8,128)S(1)}, u32[]{:S(2)}, u32[]{:S(2)}) collective-permute-start(f32[1,8,4096]{2,1,0:T(8,128)S(1)} %get-tuple-element.47), channel_id=1, source_target_pairs={{0,8},{8,16},{16,24},{24,32},{32,40},{40,48},{48,56},{56,0},{1,9},... | collective-permute-start | bytes 393224 | tf_op jit(solution)/shard_map/ppermute | solution.py:27
  192.2 15.6 %collective-permute-start.12 = (f32[1,8,4096]{2,1,0:T(8,128)S(1)}, f32[1,8,4096]{2,1,0:T(8,128)S(1)}, u32[]{:S(2)}, u32[]{:S(2)}) collective-permute-start(f32[1,8,4096]{2,1,0:T(8,128)S(1)} %get-tuple-element.32), channel_id=1, source_target_pairs={{8,0},{16,8},{24,16},{32,24},{40,32},{48,40},{56,48},{0,56},{9,1},... | collective-permute-start | bytes 393224 | tf_op jit(solution)/shard_map/ppermute | solution.py:30
  196.2 11.6 %collective-permute-start.13 = (f32[1,8,4096]{2,1,0:T(8,128)S(1)}, f32[1,8,4096]{2,1,0:T(8,128)S(1)}, u32[]{:S(2)}, u32[]{:S(2)}) collective-permute-start(f32[1,8,4096]{2,1,0:T(8,128)S(1)} %get-tuple-element.31), channel_id=1, source_target_pairs={{0,8},{8,16},{16,24},{24,32},{32,40},{40,48},{48,56},{56,0},{1,9},... | collective-permute-start | bytes 393224 | tf_op jit(solution)/shard_map/ppermute | solution.py:27
  198.4 17.4 %collective-permute-start.31 = (f32[10,1,4096]{2,1,0:T(1,128)S(1)}, f32[10,1,4096]{2,1,0:T(1,128)S(1)}, u32[]{:S(2)}, u32[]{:S(2)}) collective-permute-start(f32[10,1,4096]{2,1,0:T(1,128)S(1)} %get-tuple-element.22), channel_id=1, source_target_pairs={{0,1},{1,2},{2,3},{3,4},{4,5},{5,6},{6,7},{7,0},{8,9},{9,10},{10,1... | collective-permute-start | bytes 491528 | tf_op jit(solution)/shard_map/ppermute | solution.py:27
  205.9 10.0 %collective-permute-start.30 = (f32[10,1,4096]{2,1,0:T(1,128)S(1)}, f32[10,1,4096]{2,1,0:T(1,128)S(1)}, u32[]{:S(2)}, u32[]{:S(2)}) collective-permute-start(f32[10,1,4096]{2,1,0:T(1,128)S(1)} %get-tuple-element.21), channel_id=1, source_target_pairs={{1,0},{2,1},{3,2},{4,3},{5,4},{6,5},{7,6},{0,7},{9,8},{10,9},{11,1... | collective-permute-start | bytes 491528 | tf_op jit(solution)/shard_map/ppermute | solution.py:30
  208.1 9.3 %collective-permute-start.15 = (f32[10,1,4096]{2,1,0:T(1,128)S(1)}, f32[10,1,4096]{2,1,0:T(1,128)S(1)}, u32[]{:S(2)}, u32[]{:S(2)}) collective-permute-start(f32[10,1,4096]{2,1,0:T(1,128)S(1)} %get-tuple-element.14), channel_id=1, source_target_pairs={{0,1},{1,2},{2,3},{3,4},{4,5},{5,6},{6,7},{7,0},{8,9},{9,10},{10,1... | collective-permute-start | bytes 491528 | tf_op jit(solution)/shard_map/ppermute | solution.py:27
  213.9 10.6 %collective-permute-start.14 = (f32[10,1,4096]{2,1,0:T(1,128)S(1)}, f32[10,1,4096]{2,1,0:T(1,128)S(1)}, u32[]{:S(2)}, u32[]{:S(2)}) collective-permute-start(f32[10,1,4096]{2,1,0:T(1,128)S(1)} %get-tuple-element.13), channel_id=1, source_target_pairs={{1,0},{2,1},{3,2},{4,3},{5,4},{6,5},{7,6},{0,7},{9,8},{10,9},{11,1... | collective-permute-start | bytes 491528 | tf_op jit(solution)/shard_map/ppermute | solution.py:30
  (3 other events, 4.9 us)
where the time goes:
time: 231 us; the launch traced here: 227 us
  starting transfers between devices  134 us (58%)
  blocking collectives  48.3 us (21%)
  other arithmetic  13.9 us (6%)
  waiting for transfers between devices  13.6 us (6%)
  local copies, waits for them, and re-layouts  11.1 us (5%)
  between operations  5.84 us (3%)
    ppermute x16, starting transfers between devices, extended(): lax.ppermute(lax.slice_in_dim(block, block.shape[dim] - width, None, axis...  84 us
    ppermute x16, starting transfers between devices, extended(): lax.ppermute(lax.slice_in_dim(block, 0, width, axis=dim), axis, backward)  50.3 us
    psum x1, blocking collectives, spread_2(): return lax.psum(block, axis)  48.3 us
    ppermute x16, waiting for transfers between devices, extended(): lax.ppermute(lax.slice_in_dim(block, 0, width, axis=dim), axis, backward)  13.6 us
    another operation x8, local copies, waits for them, and re-layouts, body(): jnp.tile(source.astype(jnp.float32), (1, 1, held))  5.96 us
  transfers between devices with their start and end apart: 32, of which 5 were waited for; matrix products, arithmetic and copies ran while one was open for 5% of the time, Pallas kernels for 0%

commit v1 on v0

v1 whole, which is shorter than its diff:
```python
import functools

import jax
import jax.numpy as jnp
from jax import lax
from jax.experimental import pallas as pl
from jax.experimental.pallas import tpu as pltpu
from jax.sharding import PartitionSpec as P

NZ = 32
NSRC = 4
ZLO = 3
LANES = 128
PACK = LANES // NZ
GROUPS = 8
HALO = 4
BLK = 8
EXT = BLK + 2 * HALO
MESH = pl.DeviceIdType.MESH

C = (1.021021021021021, -1.7357357357357357, 1.4753753753753753, -1.254069069069069, 1.0659587087087088)
IN_B = (C[0] - C[2] + C[4], C[1] - 3 * C[3], 2 * C[2] - 8 * C[4], 4 * C[3], 8 * C[4])
IN_S = tuple(a * (-1.0 / 6.0) ** k for k, a in enumerate(IN_B))
LEAD = IN_S[4]
REL = tuple(a / LEAD for a in IN_S)

DIRS = tuple((ax, ay) for ax in (-1, 0, 1) for ay in (-1, 0, 1) if (ax, ay) != (0, 0))


def src_range(a, width):
    return {-1: slice(HALO, HALO + width), 0: slice(HALO, HALO + BLK), 1: slice(HALO + BLK - width, HALO + BLK)}[a]


def dst_range(a, width):
    return {-1: slice(HALO + BLK, HALO + BLK + width), 0: slice(HALO, HALO + BLK), 1: slice(HALO - width, HALO)}[a]


def kernel(
    nx, nsx, nsy,
    owner, slot, orb_hbm, out,
    inb, tall, phi, gx, gz, pp, pt, rho, wa, wb,
    in_sem, xs, xr, zs, zr, ps, pr, hs, hr,
):
    orb = lax.axis_index("orb")
    mx, mz = orb // ZLO, orb % ZLO
    sx, sy = lax.axis_index("sx"), lax.axis_index("sy")

    def near(ax, ay):
        return {"sx": lax.rem(sx + ax + nsx, nsx), "sy": lax.rem(sy + ay + nsy, nsy)}

    def x_peer(d):
        return {"orb": lax.rem(mx + d, nx) * ZLO + mz}

    def z_peer(d):
        return {"orb": mx * ZLO + lax.rem(mz + d, ZLO)}

    load = pltpu.make_async_copy(orb_hbm, inb, in_sem)
    load.start()
    barrier = pltpu.get_barrier_semaphore()
    peers = [near(*d) for d in DIRS] + [x_peer(d) for d in range(1, nx)] + [z_peer(d) for d in range(1, ZLO)]
    for peer in peers:
        pl.semaphore_signal(barrier, inc=1, device_id=peer, device_id_type=MESH)
    load.wait()

    lane = lax.broadcasted_iota(jnp.int32, (BLK, LANES), 1)
    part, cell = lane // NZ, lane % NZ

    cand = jnp.zeros((BLK, BLK, LANES), jnp.float32)
    mine = part + orb * (2 * GROUPS * PACK)
    wanted = [owner[s // 2, s % 2] * (2 * GROUPS * PACK) + slot[s // 2, s % 2] for s in range(NSRC)]
    got = [jnp.zeros((BLK, BLK, LANES), jnp.float32) for s in range(NSRC)]
    for g in range(2 * GROUPS):
        row = inb[:, :, g * LANES : (g + 1) * LANES].astype(jnp.float32)
        for s in range(NSRC):
            got[s] = jnp.where((mine + g * PACK == wanted[s])[None], row, got[s])
    for s in range(NSRC):
        m = got[s] + pltpu.roll(got[s], NZ, 2)
        m = m + pltpu.roll(m, 2 * NZ, 2)
        cand = jnp.where((part == s)[None], m, cand)
    gx[mx] = cand.astype(jnp.bfloat16)

    def relay(x, carry):
        for g in range(2 * GROUPS):
            tall[x, :, g, :] = inb[x, :, g * LANES : (g + 1) * LANES].astype(jnp.float32)
        for h in range(2):
            phi[h, HALO + x, HALO : HALO + BLK] = tall[x, :, h * GROUPS : (h + 1) * GROUPS, :].astype(jnp.bfloat16)
        return carry

    lax.fori_loop(0, BLK, relay, 0)

    pl.semaphore_wait(barrier, len(peers))

    x_copies = [
        pltpu.make_async_remote_copy(gx.at[mx], gx.at[mx], xs.at[d - 1], xr.at[d - 1], device_id=x_peer(d), device_id_type=MESH)
        for d in range(1, nx)
    ]
    for copy in x_copies:
        copy.start()

    def halo_copies(h):
        copies = []
        for k, (ax, ay) in enumerate(DIRS):
            width = HALO - 1 if ax and ay else HALO
            copies.append(
                pltpu.make_async_remote_copy(
                    phi.at[h, src_range(ax, width), src_range(ay, width)],
                    phi.at[h, dst_range(ax, width), dst_range(ay, width)],
                    hs.at[h, k], hr.at[h, k], device_id=near(ax, ay), device_id_type=MESH,
                )
            )
        return copies

    first, second = halo_copies(0), halo_copies(1)
    for copy in first:
        copy.start()

    for copy in x_copies:
        copy.wait_recv()
    mid = gx[0].astype(jnp.float32)
    for x in range(1, nx):
        mid = mid + gx[x].astype(jnp.float32)
    gz[mz] = mid.astype(jnp.bfloat16)
    z_copies = [
        pltpu.make_async_remote_copy(gz.at[mz], gz.at[mz], zs.at[d - 1], zr.at[d - 1], device_id=z_peer(d), device_id_type=MESH)
        for d in range(1, ZLO)
    ]
    for copy in z_copies:
        copy.start()
    for copy in z_copies:
        copy.wait_recv()
    mid = gz[0].astype(jnp.float32)
    for z in range(1, ZLO):
        mid = mid + gz[z].astype(jnp.float32)
    pp[1, HALO : HALO + BLK] = mid.astype(jnp.bfloat16)
    p_copies = [
        pltpu.make_async_remote_copy(
            pp.at[1, src_range(ax, HALO)], pp.at[1 - ay, dst_range(ax, HALO)],
            ps.at[k], pr.at[k], device_id=near(ax, ay), device_id_type=MESH,
        )
        for k, (ax, ay) in enumerate(DIRS)
    ]
    for copy in p_copies:
        copy.start()
    for copy in second:
        copy.start()
    for copy in p_copies:
        copy.wait_recv()

    def expand(x, carry):
        for b in range(3):
            t = pp[b, x].astype(jnp.float32)
            for s in range(NSRC):
                m = jnp.where(part == s, t, 0.0)
                m = m + pltpu.roll(m, NZ, 1)
                m = m + pltpu.roll(m, 2 * NZ, 1)
                pt[s, x, b * BLK : (b + 1) * BLK, :] = m
        return carry

    lax.fori_loop(0, EXT, expand, 0)

    up = (cell != 0).astype(jnp.float32)[None]
    down = (cell != NZ - 1).astype(jnp.float32)[None]

    def level(k, s, src, write):
        n = EXT - 2 * k
        rows = slice(k - 1, k + n + 1)
        inner = slice(k, k + n)

        def step(x, carry):
            diag, here = carry
            after = src(x + 1, rows)
            diag_here = here[: n + 1] + after[1:]
            mid = here[1 : n + 1]
            total = diag + diag_here[:n]
            total = total + (pltpu.roll(mid, 1, 2) * up + pltpu.roll(mid, LANES - 1, 2) * down)
            write(x, total + REL[4 - k] * rho[s, x, inner])
            return diag_here[1:], after

        here = src(k, rows)
        diag = src(k - 1, inner) + here[2:]
        lax.fori_loop(k, k + n, step, (diag, here))

    def half(h):
        lo = h * GROUPS

        def density(x, carry):
            row = phi[h, x].astype(jnp.float32)
            for s in range(NSRC):
                for y in range(EXT):
                    rho[s, x, y] = row[y] * pt[s, x, y + HALO : y + HALO + 1, :]
            tall[x // 2, pl.ds((x % 2) * HALO, HALO), lo : lo + GROUPS, :] = jnp.zeros((HALO, GROUPS, LANES), jnp.float32)
            return carry

        lax.fori_loop(0, EXT, density, 0)

        def source(s, carry):
            def to(ref, k):
                def write(x, value):
                    ref[x, k : EXT - k] = value

                return write

            def finish(x, value):
                for y in range(BLK):
                    term = value[y] * pt[s, x, y + 2 * HALO : y + 2 * HALO + 1, :]
                    tall[x - HALO, y, lo : lo + GROUPS, :] = tall[x - HALO, y, lo : lo + GROUPS, :] + term

            level(1, s, lambda x, r: rho[s, x, r], to(wa, 1))
            level(2, s, lambda x, r: wa[x, r], to(wb, 2))
            level(3, s, lambda x, r: wb[x, r], to(wa, 3))
            level(4, s, lambda x, r: wa[x, r], finish)
            return carry

        lax.fori_loop(0, NSRC, source, 0)

        def store(x, carry):
            for g in range(lo, lo + GROUPS):
                out[x, :, g * LANES : (g + 1) * LANES] = tall[x, :, g, :] * (-LEAD)
            return carry

        lax.fori_loop(0, BLK, store, 0)

    for copy in first:
        copy.wait_recv()
    half(0)
    for copy in second:
        copy.wait_recv()
    half(1)
    for copy in x_copies + z_copies + p_copies + first + second:
        copy.wait_send()


def solution(mesh):
    nx, nsx, nsy = mesh.shape["orb"] // ZLO, mesh.shape["sx"], mesh.shape["sy"]

    def body(orbitals, src_owner, src_slot):
        f32, bf16 = jnp.float32, jnp.bfloat16
        dma = pltpu.SemaphoreType.DMA
        return pl.pallas_call(
            functools.partial(kernel, nx, nsx, nsy),
            out_shape=jax.ShapeDtypeStruct(orbitals.shape, f32),
            in_specs=[
                pl.BlockSpec(memory_space=pltpu.SMEM),
                pl.BlockSpec(memory_space=pltpu.SMEM),
                pl.BlockSpec(memory_space=pl.ANY),
            ],
            out_specs=pl.BlockSpec(memory_space=pltpu.VMEM),
            scratch_shapes=[
                pltpu.VMEM(orbitals.shape, bf16),
                pltpu.VMEM((BLK, BLK, 2 * GROUPS, LANES), f32),
                pltpu.VMEM((2, EXT, EXT, GROUPS, LANES), bf16),
                pltpu.VMEM((nx, BLK, BLK, LANES), bf16),
                pltpu.VMEM((ZLO, BLK, BLK, LANES), bf16),
                pltpu.VMEM((3, EXT, BLK, LANES), bf16),
                pltpu.VMEM((NSRC, EXT, 3 * BLK, LANES), f32),
                pltpu.VMEM((NSRC, EXT, EXT, GROUPS, LANES), f32),
                pltpu.VMEM((EXT, EXT, GROUPS, LANES), f32),
                pltpu.VMEM((EXT, EXT, GROUPS, LANES), f32),
                dma,
                dma((max(nx - 1, 1),)), dma((max(nx - 1, 1),)),
                dma((ZLO - 1,)), dma((ZLO - 1,)),
                dma((8,)), dma((8,)),
                dma((2, 8)), dma((2, 8)),
            ],
            compiler_params=pltpu.CompilerParams(collective_id=0, has_side_effects=True),
        )(src_owner, src_slot, orbitals)

    return jax.shard_map(
        body, mesh=mesh, in_specs=(P("sx", "sy", "orb"), P(), P()), out_specs=P("sx", "sy", "orb"), check_vma=False
    )
```

time: 231 us -> 70.5 us (0.31); the launches traced: 227 us -> 70.3 us
  starting transfers between devices: 134 us -> 0 us
  Pallas kernels: 0 us -> 68.4 us
  blocking collectives: 48.3 us -> 0 us
  other arithmetic: 13.9 us -> 0 us
  waiting for transfers between devices: 13.6 us -> 0 us
  local copies, waits for them, and re-layouts: 11.1 us -> 1.87 us
  between operations: 5.84 us -> 0.01 us
    ppermute x32 -> x0, starting transfers between devices: 134 us -> none  [the longest x16 84 us: extended(): lax.ppermute(lax.slice_in_dim(block, block.shape[dim] - width, None, axis...]
    pallas_call x0 -> x1, Pallas kernels: none -> 68.4 us  [body(): pl.pallas_call(functools.partial(kernel, nx, nsx, nsy), out_shape=jax.Sha...]
    psum x1 -> x0, blocking collectives: 48.3 us -> none  [spread_2(): return lax.psum(block, axis)]
    ppermute x32 -> x0, waiting for transfers between devices: 13.6 us -> none  [the longest x16 13.6 us: extended(): lax.ppermute(lax.slice_in_dim(block, 0, width, axis=dim), axis, backward)]
    another operation x8 -> x0, local copies, waits for them, and re-layouts: 5.96 us -> none  [body(): jnp.tile(source.astype(jnp.float32), (1, 1, held))]
    slice x14 -> x0, local copies, waits for them, and re-layouts: 5.18 us -> none  [the longest x6 2.1 us: screened(): core[..., 1:]]
    sub x5 -> x0, other arithmetic: 4.25 us -> none  [the longest x4 3.12 us: potential(): t_next = 2.0 * screened(widen_one(t_cur)) - t_prev]
    add x3 -> x0, other arithmetic: 2.96 us -> none  [the longest x2 2.96 us: potential(): total = total + cheb_coeffs[order] * t_next]
  transfers between devices with their start and end apart: 32 -> 0, of which waited for: 5 -> 0; matrix products, arithmetic and copies ran while one was open for 5% -> 0% of each run, Pallas kernels for 0% -> 0%
where the time goes in v1:
time: 70.5 us; the launch traced here: 70.3 us
  Pallas kernels  68.4 us (97%)
  local copies, waits for them, and re-layouts  1.87 us (3%)
    pallas_call x1, Pallas kernels, body(): pl.pallas_call(functools.partial(kernel, nx, nsx, nsy), out_shape=jax.Sha...  68.4 us
    unnamed x1, local copies, waits for them, and re-layouts  1.87 us

profile of v1, /device:TPU:1, one launch (start us, length us, event | category | flops | bytes accessed | tf_op | source)
XLA Modules:
  0.0 70.3 jit_solution(5810953679077086592)
XLA Ops:
  0.0 68.4 %shard_map.37 = f32[8,8,2048]{2,1,0:T(8,128)} custom-call(s32[2,2]{1,0:T(2,128)} %owner.1, s32[2,2]{1,0:T(2,128)} %slot.1, bf16[8,8,2048]{2,1,0:T(8,128)(2,1)} %orb_hbm.1), custom_call_target="tpu_custom_call" | custom-call | tf_op jit(solution)/shard_map/pallas_call | solution.py:239
  68.4 1.9 %copy.5 = f32[8,8,2048]{2,1,0:T(8,128)} copy(f32[8,8,2048]{2,1,0:T(8,128)} %shard_map.37) | data formatting | bytes 1048576

commit v2 on v1

--- a/solution.py
+++ b/solution.py
@@ -1,7 +1,9 @@
 import functools
+import math
 
 import jax
 import jax.numpy as jnp
+import numpy as np
 from jax import lax
 from jax.experimental import pallas as pl
 from jax.experimental.pallas import tpu as pltpu
@@ -24,6 +26,26 @@
 LEAD = IN_S[4]
 REL = tuple(a / LEAD for a in IN_S)
 
+UNROLL = 2
+TERMS = 4
+
+
+def constants():
+    chain = np.eye(NZ, k=1) + np.eye(NZ, k=-1)
+    q = []
+    for m in range(TERMS):
+        z = sum(math.comb(m + n, m) * REL[m + n] * np.linalg.matrix_power(chain, n) for n in range(5 - m))
+        q.append(np.kron(np.eye(PACK), z))
+    q = np.concatenate(q).astype(np.float32)
+    high = q.astype(jnp.bfloat16)
+    low = (q - high.astype(np.float32)).astype(jnp.bfloat16)
+    same = np.tile(np.eye(NZ), (PACK, PACK))
+    into = [same * (np.arange(LANES)[None] // NZ == s) for s in range(NSRC)]
+    gather = np.concatenate(into).astype(jnp.bfloat16)
+    spread = np.concatenate([one.T for one in into]).astype(jnp.bfloat16)
+    return np.concatenate([high, low, gather, spread], axis=1)
+
+
 DIRS = tuple((ax, ay) for ax in (-1, 0, 1) for ay in (-1, 0, 1) if (ax, ay) != (0, 0))
 
 
@@ -37,9 +59,9 @@
 
 def kernel(
     nx, nsx, nsy,
-    owner, slot, orb_hbm, out,
-    inb, tall, phi, gx, gz, pp, pt, rho, wa, wb,
-    in_sem, xs, xr, zs, zr, ps, pr, hs, hr,
+    owner, slot, orb_hbm, mats_hbm, out,
+    inb, mats, tall, phi, gx, gz, pp, pt, rho, u1, u2, u3, u4, xh, xl, res,
+    in_sem, mat_sem, xs, xr, zs, zr, ps, pr, hs, hr,
 ):
     orb = lax.axis_index("orb")
     mx, mz = orb // ZLO, orb % ZLO
@@ -56,6 +78,8 @@
 
     load = pltpu.make_async_copy(orb_hbm, inb, in_sem)
     load.start()
+    load_mats = pltpu.make_async_copy(mats_hbm, mats, mat_sem)
+    load_mats.start()
     barrier = pltpu.get_barrier_semaphore()
     peers = [near(*d) for d in DIRS] + [x_peer(d) for d in range(1, nx)] + [z_peer(d) for d in range(1, ZLO)]
     for peer in peers:
@@ -63,9 +87,8 @@
     load.wait()
 
     lane = lax.broadcasted_iota(jnp.int32, (BLK, LANES), 1)
-    part, cell = lane // NZ, lane % NZ
-
-    cand = jnp.zeros((BLK, BLK, LANES), jnp.float32)
+    part = lane // NZ
+
     mine = part + orb * (2 * GROUPS * PACK)
     wanted = [owner[s // 2, s % 2] * (2 * GROUPS * PACK) + slot[s // 2, s % 2] for s in range(NSRC)]
     got = [jnp.zeros((BLK, BLK, LANES), jnp.float32) for s in range(NSRC)]
@@ -73,17 +96,18 @@
         row = inb[:, :, g * LANES : (g + 1) * LANES].astype(jnp.float32)
         for s in range(NSRC):
             got[s] = jnp.where((mine + g * PACK == wanted[s])[None], row, got[s])
-    for s in range(NSRC):
-        m = got[s] + pltpu.roll(got[s], NZ, 2)
-        m = m + pltpu.roll(m, 2 * NZ, 2)
-        cand = jnp.where((part == s)[None], m, cand)
-    gx[mx] = cand.astype(jnp.bfloat16)
+    load_mats.wait()
+    rows = jnp.concatenate([v.reshape(BLK * BLK, LANES).astype(jnp.bfloat16) for v in got], axis=1)
+    cand = jnp.dot(rows, mats[:, 2 * LANES : 3 * LANES], preferred_element_type=jnp.float32)
+    gx[mx] = cand.reshape(BLK, BLK, LANES).astype(jnp.bfloat16)
 
     def relay(x, carry):
         for g in range(2 * GROUPS):
-            tall[x, :, g, :] = inb[x, :, g * LANES : (g + 1) * LANES].astype(jnp.float32)
+            tall[x, pl.ds(g, BLK, stride=2 * GROUPS), :] = inb[x, :, g * LANES : (g + 1) * LANES].astype(jnp.float32)
         for h in range(2):
-            phi[h, HALO + x, HALO : HALO + BLK] = tall[x, :, h * GROUPS : (h + 1) * GROUPS, :].astype(jnp.bfloat16)
+            for y in range(BLK):
+                at = (2 * y + h) * GROUPS
+                phi[h, HALO + x, HALO + y] = tall[x, at : at + GROUPS, :].astype(jnp.bfloat16)
         return carry
 
     lax.fori_loop(0, BLK, relay, 0)
@@ -146,39 +170,31 @@
     for copy in p_copies:
         copy.wait_recv()
 
-    def expand(x, carry):
+    every = pp[...].astype(jnp.float32).reshape(3 * EXT * BLK, LANES).astype(jnp.bfloat16)
+    for s in range(NSRC):
+        wide = jnp.dot(every, mats[s * LANES : (s + 1) * LANES, 3 * LANES :], preferred_element_type=jnp.float32)
+        wide = wide.reshape(3, EXT, BLK, LANES)
         for b in range(3):
-            t = pp[b, x].astype(jnp.float32)
-            for s in range(NSRC):
-                m = jnp.where(part == s, t, 0.0)
-                m = m + pltpu.roll(m, NZ, 1)
-                m = m + pltpu.roll(m, 2 * NZ, 1)
-                pt[s, x, b * BLK : (b + 1) * BLK, :] = m
-        return carry
-
-    lax.fori_loop(0, EXT, expand, 0)
-
-    up = (cell != 0).astype(jnp.float32)[None]
-    down = (cell != NZ - 1).astype(jnp.float32)[None]
-
-    def level(k, s, src, write):
+            pt[s, :, b * BLK : (b + 1) * BLK, :] = wide[b]
+
+    def level(k, src, dst):
         n = EXT - 2 * k
         rows = slice(k - 1, k + n + 1)
         inner = slice(k, k + n)
 
         def step(x, carry):
             diag, here = carry
-            after = src(x + 1, rows)
+            after = src[x + 1, rows]
             diag_here = here[: n + 1] + after[1:]
-            mid = here[1 : n + 1]
-            total = diag + diag_here[:n]
-            total = total + (pltpu.roll(mid, 1, 2) * up + pltpu.roll(mid, LANES - 1, 2) * down)
-            write(x, total + REL[4 - k] * rho[s, x, inner])
+            dst[x, inner] = diag + diag_here[:n]
             return diag_here[1:], after
 
-        here = src(k, rows)
-        diag = src(k - 1, inner) + here[2:]
-        lax.fori_loop(k, k + n, step, (diag, here))
+        here = src[k, rows]
+        diag = src[k - 1, inner] + here[2:]
+        lax.fori_loop(k, k + n, step, (diag, here), unroll=UNROLL)
+
+    core = slice(HALO, HALO + BLK)
+    plane = BLK * GROUPS
 
     def half(h):
         lo = h * GROUPS
@@ -188,37 +204,47 @@
             for s in range(NSRC):
                 for y in range(EXT):
                     rho[s, x, y] = row[y] * pt[s, x, y + HALO : y + HALO + 1, :]
-            tall[x // 2, pl.ds((x % 2) * HALO, HALO), lo : lo + GROUPS, :] = jnp.zeros((HALO, GROUPS, LANES), jnp.float32)
             return carry
 
         lax.fori_loop(0, EXT, density, 0)
 
         def source(s, carry):
-            def to(ref, k):
-                def write(x, value):
-                    ref[x, k : EXT - k] = value
-
-                return write
-
-            def finish(x, value):
-                for y in range(BLK):
-                    term = value[y] * pt[s, x, y + 2 * HALO : y + 2 * HALO + 1, :]
-                    tall[x - HALO, y, lo : lo + GROUPS, :] = tall[x - HALO, y, lo : lo + GROUPS, :] + term
-
-            level(1, s, lambda x, r: rho[s, x, r], to(wa, 1))
-            level(2, s, lambda x, r: wa[x, r], to(wb, 2))
-            level(3, s, lambda x, r: wb[x, r], to(wa, 3))
-            level(4, s, lambda x, r: wa[x, r], finish)
+            level(1, rho.at[s], u1)
+            level(2, u1, u2)
+            level(3, u2, u3)
+            level(4, u3, u4.at[s])
+
+            def split(x, carry):
+                at = pl.ds(pl.multiple_of(x * plane, plane), plane)
+                for m, ref in enumerate((rho.at[s], u1, u2, u3)):
+                    value = ref[HALO + x, core].reshape(plane, LANES)
+                    high = value.astype(jnp.bfloat16)
+                    xh[at, m * LANES : (m + 1) * LANES] = high
+                    xl[at, m * LANES : (m + 1) * LANES] = (value - high.astype(jnp.float32)).astype(jnp.bfloat16)
+                return carry
+
+            lax.fori_loop(0, BLK, split, 0, unroll=2)
+            both = jnp.dot(xh[...], mats[:, : 2 * LANES], preferred_element_type=jnp.float32)
+            rest = jnp.dot(xl[...], mats[:, :LANES], preferred_element_type=jnp.float32)
+            res[s] = both[:, :LANES] + both[:, LANES:] + rest
             return carry
 
         lax.fori_loop(0, NSRC, source, 0)
 
-        def store(x, carry):
+        def finish(x, carry):
+            for y in range(BLK):
+                total = jnp.zeros((GROUPS, LANES), jnp.float32)
+                for s in range(NSRC):
+                    at = pl.ds(pl.multiple_of(x * plane + y * GROUPS, GROUPS), GROUPS)
+                    value = res[s, at, :] + u4[s, HALO + x, HALO + y]
+                    total = total + value * pt[s, x + HALO, y + 2 * HALO : y + 2 * HALO + 1, :]
+                at = (2 * y + h) * GROUPS
+                tall[x, at : at + GROUPS, :] = total * (-LEAD)
             for g in range(lo, lo + GROUPS):
-                out[x, :, g * LANES : (g + 1) * LANES] = tall[x, :, g, :] * (-LEAD)
+                out[x, :, g * LANES : (g + 1) * LANES] = tall[x, pl.ds(g, BLK, stride=2 * GROUPS), :]
             return carry
 
-        lax.fori_loop(0, BLK, store, 0)
+        lax.fori_loop(0, BLK, finish, 0)
 
     for copy in first:
         copy.wait_recv()
@@ -235,6 +261,7 @@
 
     def body(orbitals, src_owner, src_slot):
         f32, bf16 = jnp.float32, jnp.bfloat16
+        mats = constants()
         dma = pltpu.SemaphoreType.DMA
         return pl.pallas_call(
             functools.partial(kernel, nx, nsx, nsy),
@@ -243,11 +270,13 @@
                 pl.BlockSpec(memory_space=pltpu.SMEM),
                 pl.BlockSpec(memory_space=pltpu.SMEM),
                 pl.BlockSpec(memory_space=pl.ANY),
+                pl.BlockSpec(memory_space=pl.ANY),
             ],
             out_specs=pl.BlockSpec(memory_space=pltpu.VMEM),
             scratch_shapes=[
                 pltpu.VMEM(orbitals.shape, bf16),
-                pltpu.VMEM((BLK, BLK, 2 * GROUPS, LANES), f32),
+                pltpu.VMEM(mats.shape, bf16),
+                pltpu.VMEM((BLK, BLK * 2 * GROUPS, LANES), f32),
                 pltpu.VMEM((2, EXT, EXT, GROUPS, LANES), bf16),
                 pltpu.VMEM((nx, BLK, BLK, LANES), bf16),
                 pltpu.VMEM((ZLO, BLK, BLK, LANES), bf16),
@@ -256,14 +285,19 @@
                 pltpu.VMEM((NSRC, EXT, EXT, GROUPS, LANES), f32),
                 pltpu.VMEM((EXT, EXT, GROUPS, LANES), f32),
                 pltpu.VMEM((EXT, EXT, GROUPS, LANES), f32),
-                dma,
+                pltpu.VMEM((EXT, EXT, GROUPS, LANES), f32),
+                pltpu.VMEM((NSRC, EXT, EXT, GROUPS, LANES), f32),
+                pltpu.VMEM((BLK * BLK * GROUPS, TERMS * LANES), bf16),
+                pltpu.VMEM((BLK * BLK * GROUPS, TERMS * LANES), bf16),
+                pltpu.VMEM((NSRC, BLK * BLK * GROUPS, LANES), f32),
+                dma, dma,
                 dma((max(nx - 1, 1),)), dma((max(nx - 1, 1),)),
                 dma((ZLO - 1,)), dma((ZLO - 1,)),
                 dma((8,)), dma((8,)),
                 dma((2, 8)), dma((2, 8)),
             ],
             compiler_params=pltpu.CompilerParams(collective_id=0, has_side_effects=True),
-        )(src_owner, src_slot, orbitals)
+        )(src_owner, src_slot, orbitals, jnp.asarray(mats))
 
     return jax.shard_map(
         body, mesh=mesh, in_specs=(P("sx", "sy", "orb"), P(), P()), out_specs=P("sx", "sy", "orb"), check_vma=False

time: 70.5 us -> 42.2 us (0.60)
  Pallas kernels: 68.4 us -> 40.1 us
    pallas_call x1, Pallas kernels: 68.4 us -> 40.1 us  [body(): pl.pallas_call(functools.partial(kernel, nx, nsx, nsy), out_shape=jax.Sha...]
where the time goes in v2:
time: 42.2 us; the launch traced here: 42 us
  Pallas kernels  40.1 us (95%)
  local copies, waits for them, and re-layouts  1.87 us (4%)
    pallas_call x1, Pallas kernels, body(): pl.pallas_call(functools.partial(kernel, nx, nsx, nsy), out_shape=jax.Sha...  40.1 us
    unnamed x1, local copies, waits for them, and re-layouts  1.87 us

profile of v2, /device:TPU:1, one launch (start us, length us, event | category | flops | bytes accessed | tf_op | source)
XLA Modules:
  0.0 42.0 jit_solution(13361250963957570870)
XLA Ops:
  0.0 40.1 %shard_map.46 = f32[8,8,2048]{2,1,0:T(8,128)} custom-call(s32[2,2]{1,0:T(2,128)} %owner.1, s32[2,2]{1,0:T(2,128)} %slot.1, bf16[8,8,2048]{2,1,0:T(8,128)(2,1)} %orb_hbm.1, bf16[512,512]{1,0:T(8,128)(2,1)} %constant.2.clone.mats_hbm), custom_call_target="tpu_custom_call" | custom-call | tf_op jit(solution)/shard_map/pallas_call | solution.py:266
  40.1 1.9 %copy.6 = f32[8,8,2048]{2,1,0:T(8,128)} copy(f32[8,8,2048]{2,1,0:T(8,128)} %shard_map.46) | data formatting | bytes 1048576

commit v3 on v2

--- a/solution.py
+++ b/solution.py
@@ -11,7 +11,6 @@
 
 NZ = 32
 NSRC = 4
-ZLO = 3
 LANES = 128
 PACK = LANES // NZ
 GROUPS = 8
@@ -27,6 +26,8 @@
 REL = tuple(a / LEAD for a in IN_S)
 
 UNROLL = 2
+FIRST, REST = slice(0, None), slice(0, 0)
+SPREAD = tuple((ax, ay) for ay in (-1, 1, 0) for ax in (0, -1, 1) if (ax, ay) != (0, 0))
 TERMS = 4
 
 
@@ -58,39 +59,41 @@
 
 
 def kernel(
-    nx, nsx, nsy,
-    owner, slot, orb_hbm, mats_hbm, out,
-    inb, mats, tall, phi, gx, gz, pp, pt, rho, u1, u2, u3, u4, xh, xl, res,
-    in_sem, mat_sem, xs, xr, zs, zr, ps, pr, hs, hr,
+    norb, nsx, nsy,
+    owner_hbm, slot_hbm, orb_hbm, mats_hbm, out,
+    small, inb, mats, tall, phi, gx, pz, pt, rho, u1, u2, u3, u4, xh, xl, res,
+    in_sem, mat_sem, small_sem, xs, xr, ps, pr, hs, hr,
 ):
     orb = lax.axis_index("orb")
-    mx, mz = orb // ZLO, orb % ZLO
     sx, sy = lax.axis_index("sx"), lax.axis_index("sy")
 
     def near(ax, ay):
         return {"sx": lax.rem(sx + ax + nsx, nsx), "sy": lax.rem(sy + ay + nsy, nsy)}
 
-    def x_peer(d):
-        return {"orb": lax.rem(mx + d, nx) * ZLO + mz}
-
-    def z_peer(d):
-        return {"orb": mx * ZLO + lax.rem(mz + d, ZLO)}
-
+    def orb_peer(d):
+        return {"orb": lax.rem(orb + d, norb)}
+
+    barrier = pltpu.get_barrier_semaphore()
+    peers = [near(*d) for d in SPREAD] + [orb_peer(d) for d in range(1, norb)]
+    for peer in peers:
+        pl.semaphore_signal(barrier, inc=1, device_id=peer, device_id_type=MESH)
     load = pltpu.make_async_copy(orb_hbm, inb, in_sem)
     load.start()
     load_mats = pltpu.make_async_copy(mats_hbm, mats, mat_sem)
     load_mats.start()
-    barrier = pltpu.get_barrier_semaphore()
-    peers = [near(*d) for d in DIRS] + [x_peer(d) for d in range(1, nx)] + [z_peer(d) for d in range(1, ZLO)]
-    for peer in peers:
-        pl.semaphore_signal(barrier, inc=1, device_id=peer, device_id_type=MESH)
+    load_owner = pltpu.make_async_copy(owner_hbm, small.at[0], small_sem.at[0])
+    load_owner.start()
+    load_slot = pltpu.make_async_copy(slot_hbm, small.at[1], small_sem.at[1])
+    load_slot.start()
+    load_owner.wait()
+    load_slot.wait()
     load.wait()
 
     lane = lax.broadcasted_iota(jnp.int32, (BLK, LANES), 1)
     part = lane // NZ
 
     mine = part + orb * (2 * GROUPS * PACK)
-    wanted = [owner[s // 2, s % 2] * (2 * GROUPS * PACK) + slot[s // 2, s % 2] for s in range(NSRC)]
+    wanted = [small[0, s // 2, s % 2] * (2 * GROUPS * PACK) + small[1, s // 2, s % 2] for s in range(NSRC)]
     got = [jnp.zeros((BLK, BLK, LANES), jnp.float32) for s in range(NSRC)]
     for g in range(2 * GROUPS):
         row = inb[:, :, g * LANES : (g + 1) * LANES].astype(jnp.float32)
@@ -99,7 +102,9 @@
     load_mats.wait()
     rows = jnp.concatenate([v.reshape(BLK * BLK, LANES).astype(jnp.bfloat16) for v in got], axis=1)
     cand = jnp.dot(rows, mats[:, 2 * LANES : 3 * LANES], preferred_element_type=jnp.float32)
-    gx[mx] = cand.reshape(BLK, BLK, LANES).astype(jnp.bfloat16)
+    for x in range(BLK):
+        tall[0, pl.ds(x, BLK, stride=BLK), :] = cand[x * BLK : (x + 1) * BLK]
+    gx[orb] = tall[0, : BLK * BLK].reshape(BLK, BLK, LANES).astype(jnp.bfloat16)
 
     def relay(x, carry):
         for g in range(2 * GROUPS):
@@ -115,8 +120,10 @@
     pl.semaphore_wait(barrier, len(peers))
 
     x_copies = [
-        pltpu.make_async_remote_copy(gx.at[mx], gx.at[mx], xs.at[d - 1], xr.at[d - 1], device_id=x_peer(d), device_id_type=MESH)
-        for d in range(1, nx)
+        pltpu.make_async_remote_copy(
+            gx.at[orb], gx.at[orb], xs.at[d - 1], xr.at[d - 1], device_id=orb_peer(d), device_id_type=MESH
+        )
+        for d in range(1, norb)
     ]
     for copy in x_copies:
         copy.start()
@@ -135,42 +142,34 @@
         return copies
 
     first, second = halo_copies(0), halo_copies(1)
-    for copy in first:
-        copy.start()
-
+    for copy in first[FIRST]:
+        copy.start()
     for copy in x_copies:
         copy.wait_recv()
     mid = gx[0].astype(jnp.float32)
-    for x in range(1, nx):
+    for x in range(1, norb):
         mid = mid + gx[x].astype(jnp.float32)
-    gz[mz] = mid.astype(jnp.bfloat16)
-    z_copies = [
-        pltpu.make_async_remote_copy(gz.at[mz], gz.at[mz], zs.at[d - 1], zr.at[d - 1], device_id=z_peer(d), device_id_type=MESH)
-        for d in range(1, ZLO)
-    ]
-    for copy in z_copies:
-        copy.start()
-    for copy in z_copies:
-        copy.wait_recv()
-    mid = gz[0].astype(jnp.float32)
-    for z in range(1, ZLO):
-        mid = mid + gz[z].astype(jnp.float32)
-    pp[1, HALO : HALO + BLK] = mid.astype(jnp.bfloat16)
-    p_copies = [
-        pltpu.make_async_remote_copy(
-            pp.at[1, src_range(ax, HALO)], pp.at[1 - ay, dst_range(ax, HALO)],
-            ps.at[k], pr.at[k], device_id=near(ax, ay), device_id_type=MESH,
+    pz[1, HALO : HALO + BLK] = mid.astype(jnp.bfloat16)
+    p_copies = []
+    for k, (ax, ay) in enumerate(SPREAD):
+        width = HALO - 1 if ax and ay else HALO
+        p_copies.append(
+            pltpu.make_async_remote_copy(
+                pz.at[1, src_range(ay, width)], pz.at[1 - ax, dst_range(ay, width)],
+                ps.at[k], pr.at[k], device_id=near(ax, ay), device_id_type=MESH,
+            )
         )
-        for k, (ax, ay) in enumerate(DIRS)
-    ]
     for copy in p_copies:
+        copy.start()
+    for copy in first[REST]:
         copy.start()
     for copy in second:
         copy.start()
     for copy in p_copies:
         copy.wait_recv()
 
-    every = pp[...].astype(jnp.float32).reshape(3 * EXT * BLK, LANES).astype(jnp.bfloat16)
+    every = pz[...].astype(jnp.float32)
+    every = every.reshape(3 * EXT * BLK, LANES).astype(jnp.bfloat16)
     for s in range(NSRC):
         wide = jnp.dot(every, mats[s * LANES : (s + 1) * LANES, 3 * LANES :], preferred_element_type=jnp.float32)
         wide = wide.reshape(3, EXT, BLK, LANES)
@@ -203,7 +202,7 @@
             row = phi[h, x].astype(jnp.float32)
             for s in range(NSRC):
                 for y in range(EXT):
-                    rho[s, x, y] = row[y] * pt[s, x, y + HALO : y + HALO + 1, :]
+                    rho[s, x, y] = row[y] * pt[s, y, pl.ds(x + HALO, 1), :]
             return carry
 
         lax.fori_loop(0, EXT, density, 0)
@@ -219,17 +218,18 @@
                 for m, ref in enumerate((rho.at[s], u1, u2, u3)):
                     value = ref[HALO + x, core].reshape(plane, LANES)
                     high = value.astype(jnp.bfloat16)
-                    xh[at, m * LANES : (m + 1) * LANES] = high
-                    xl[at, m * LANES : (m + 1) * LANES] = (value - high.astype(jnp.float32)).astype(jnp.bfloat16)
+                    xh[s, at, m * LANES : (m + 1) * LANES] = high
+                    xl[s, at, m * LANES : (m + 1) * LANES] = (value - high.astype(jnp.float32)).astype(jnp.bfloat16)
                 return carry
 
             lax.fori_loop(0, BLK, split, 0, unroll=2)
-            both = jnp.dot(xh[...], mats[:, : 2 * LANES], preferred_element_type=jnp.float32)
-            rest = jnp.dot(xl[...], mats[:, :LANES], preferred_element_type=jnp.float32)
-            res[s] = both[:, :LANES] + both[:, LANES:] + rest
             return carry
 
         lax.fori_loop(0, NSRC, source, 0)
+        every_row = (NSRC * BLK * plane, TERMS * LANES)
+        both = jnp.dot(xh[...].reshape(every_row), mats[:, : 2 * LANES], preferred_element_type=jnp.float32)
+        rest = jnp.dot(xl[...].reshape(every_row), mats[:, :LANES], preferred_element_type=jnp.float32)
+        res[...] = (both[:, :LANES] + both[:, LANES:] + rest).reshape(NSRC, BLK * plane, LANES)
 
         def finish(x, carry):
             for y in range(BLK):
@@ -237,7 +237,7 @@
                 for s in range(NSRC):
                     at = pl.ds(pl.multiple_of(x * plane + y * GROUPS, GROUPS), GROUPS)
                     value = res[s, at, :] + u4[s, HALO + x, HALO + y]
-                    total = total + value * pt[s, x + HALO, y + 2 * HALO : y + 2 * HALO + 1, :]
+                    total = total + value * pt[s, y + HALO, pl.ds(x + 2 * HALO, 1), :]
                 at = (2 * y + h) * GROUPS
                 tall[x, at : at + GROUPS, :] = total * (-LEAD)
             for g in range(lo, lo + GROUPS):
@@ -252,34 +252,34 @@
     for copy in second:
         copy.wait_recv()
     half(1)
-    for copy in x_copies + z_copies + p_copies + first + second:
+    for copy in x_copies + p_copies + first + second:
         copy.wait_send()
 
 
 def solution(mesh):
-    nx, nsx, nsy = mesh.shape["orb"] // ZLO, mesh.shape["sx"], mesh.shape["sy"]
+    norb, nsx, nsy = mesh.shape["orb"], mesh.shape["sx"], mesh.shape["sy"]
 
     def body(orbitals, src_owner, src_slot):
         f32, bf16 = jnp.float32, jnp.bfloat16
         mats = constants()
         dma = pltpu.SemaphoreType.DMA
         return pl.pallas_call(
-            functools.partial(kernel, nx, nsx, nsy),
+            functools.partial(kernel, norb, nsx, nsy),
             out_shape=jax.ShapeDtypeStruct(orbitals.shape, f32),
             in_specs=[
-                pl.BlockSpec(memory_space=pltpu.SMEM),
-                pl.BlockSpec(memory_space=pltpu.SMEM),
+                pl.BlockSpec(memory_space=pl.ANY),
+                pl.BlockSpec(memory_space=pl.ANY),
                 pl.BlockSpec(memory_space=pl.ANY),
                 pl.BlockSpec(memory_space=pl.ANY),
             ],
             out_specs=pl.BlockSpec(memory_space=pltpu.VMEM),
             scratch_shapes=[
+                pltpu.SMEM((2,) + src_owner.shape, jnp.int32),
                 pltpu.VMEM(orbitals.shape, bf16),
                 pltpu.VMEM(mats.shape, bf16),
                 pltpu.VMEM((BLK, BLK * 2 * GROUPS, LANES), f32),
                 pltpu.VMEM((2, EXT, EXT, GROUPS, LANES), bf16),
-                pltpu.VMEM((nx, BLK, BLK, LANES), bf16),
-                pltpu.VMEM((ZLO, BLK, BLK, LANES), bf16),
+                pltpu.VMEM((norb, BLK, BLK, LANES), bf16),
                 pltpu.VMEM((3, EXT, BLK, LANES), bf16),
                 pltpu.VMEM((NSRC, EXT, 3 * BLK, LANES), f32),
                 pltpu.VMEM((NSRC, EXT, EXT, GROUPS, LANES), f32),
@@ -287,13 +287,12 @@
                 pltpu.VMEM((EXT, EXT, GROUPS, LANES), f32),
                 pltpu.VMEM((EXT, EXT, GROUPS, LANES), f32),
                 pltpu.VMEM((NSRC, EXT, EXT, GROUPS, LANES), f32),
-                pltpu.VMEM((BLK * BLK * GROUPS, TERMS * LANES), bf16),
-                pltpu.VMEM((BLK * BLK * GROUPS, TERMS * LANES), bf16),
+                pltpu.VMEM((NSRC, BLK * BLK * GROUPS, TERMS * LANES), bf16),
+                pltpu.VMEM((NSRC, BLK * BLK * GROUPS, TERMS * LANES), bf16),
                 pltpu.VMEM((NSRC, BLK * BLK * GROUPS, LANES), f32),
-                dma, dma,
-                dma((max(nx - 1, 1),)), dma((max(nx - 1, 1),)),
-                dma((ZLO - 1,)), dma((ZLO - 1,)),
-                dma((8,)), dma((8,)),
+                dma, dma, dma((2,)),
+                dma((norb - 1,)), dma((norb - 1,)),
+                dma((len(SPREAD),)), dma((len(SPREAD),)),
                 dma((2, 8)), dma((2, 8)),
             ],
             compiler_params=pltpu.CompilerParams(collective_id=0, has_side_effects=True),

time: 42.2 us -> 39.8 us (0.943)
  the two profiles are of different devices: /device:TPU:1 before, /device:TPU:129 now
where the time goes in v3:
time: 39.8 us; the launch traced here: 39.6 us
  Pallas kernels  37.7 us (95%)
  local copies, waits for them, and re-layouts  1.87 us (5%)
    pallas_call x1, Pallas kernels, body(): pl.pallas_call(functools.partial(kernel, norb, nsx, nsy), out_shape=jax.S...  37.7 us
    unnamed x1, local copies, waits for them, and re-layouts  1.87 us

profile of v3, /device:TPU:129, one launch (start us, length us, event | category | flops | bytes accessed | tf_op | source)
XLA Modules:
  0.0 39.6 jit_solution(2452417461766784732)
XLA Ops:
  0.0 37.7 %shard_map.46 = f32[8,8,2048]{2,1,0:T(8,128)} custom-call(s32[2,2]{1,0:T(2,128)} %owner_hbm.1, s32[2,2]{1,0:T(2,128)} %slot_hbm.1, bf16[8,8,2048]{2,1,0:T(8,128)(2,1)} %orb_hbm.1, bf16[512,512]{1,0:T(8,128)(2,1)} %constant.2.clone.mats_hbm), custom_call_target="tpu_custom_call" | custom-call | tf_op jit(solution)/shard_map/pallas_call | solution.py:266
  37.7 1.9 %copy.6 = f32[8,8,2048]{2,1,0:T(8,128)} copy(f32[8,8,2048]{2,1,0:T(8,128)} %shard_map.46) | data formatting | bytes 1048576

commit v4 on v3

--- a/solution.py
+++ b/solution.py
@@ -190,10 +190,15 @@
 
         here = src[k, rows]
         diag = src[k - 1, inner] + here[2:]
-        lax.fori_loop(k, k + n, step, (diag, here), unroll=UNROLL)
+        lax.fori_loop(k, k + n, step, (diag, here), unroll=n)
 
     core = slice(HALO, HALO + BLK)
     plane = BLK * GROUPS
+
+    def product(s):
+        both = jnp.dot(xh[s], mats[:, : 2 * LANES], preferred_element_type=jnp.float32)
+        rest = jnp.dot(xl[s], mats[:, :LANES], preferred_element_type=jnp.float32)
+        res[s] = both[:, :LANES] + both[:, LANES:] + rest
 
     def half(h):
         lo = h * GROUPS
@@ -205,13 +210,15 @@
                     rho[s, x, y] = row[y] * pt[s, y, pl.ds(x + HALO, 1), :]
             return carry
 
-        lax.fori_loop(0, EXT, density, 0)
-
-        def source(s, carry):
+        lax.fori_loop(0, EXT, density, 0, unroll=2)
+
+        for s in range(NSRC):
             level(1, rho.at[s], u1)
             level(2, u1, u2)
             level(3, u2, u3)
             level(4, u3, u4.at[s])
+            if s:
+                product(s - 1)
 
             def split(x, carry):
                 at = pl.ds(pl.multiple_of(x * plane, plane), plane)
@@ -222,14 +229,8 @@
                     xl[s, at, m * LANES : (m + 1) * LANES] = (value - high.astype(jnp.float32)).astype(jnp.bfloat16)
                 return carry
 
-            lax.fori_loop(0, BLK, split, 0, unroll=2)
-            return carry
-
-        lax.fori_loop(0, NSRC, source, 0)
-        every_row = (NSRC * BLK * plane, TERMS * LANES)
-        both = jnp.dot(xh[...].reshape(every_row), mats[:, : 2 * LANES], preferred_element_type=jnp.float32)
-        rest = jnp.dot(xl[...].reshape(every_row), mats[:, :LANES], preferred_element_type=jnp.float32)
-        res[...] = (both[:, :LANES] + both[:, LANES:] + rest).reshape(NSRC, BLK * plane, LANES)
+            lax.fori_loop(0, BLK, split, 0, unroll=BLK)
+        product(NSRC - 1)
 
         def finish(x, carry):
             for y in range(BLK):
@@ -244,7 +245,7 @@
                 out[x, :, g * LANES : (g + 1) * LANES] = tall[x, pl.ds(g, BLK, stride=2 * GROUPS), :]
             return carry
 
-        lax.fori_loop(0, BLK, finish, 0)
+        lax.fori_loop(0, BLK, finish, 0, unroll=2)
 
     for copy in first:
         copy.wait_recv()
@@ -265,7 +266,7 @@
         dma = pltpu.SemaphoreType.DMA
         return pl.pallas_call(
             functools.partial(kernel, norb, nsx, nsy),
-            out_shape=jax.ShapeDtypeStruct(orbitals.shape, f32),
+            out_shape=pltpu.VMEM(orbitals.shape, f32),
             in_specs=[
                 pl.BlockSpec(memory_space=pl.ANY),
                 pl.BlockSpec(memory_space=pl.ANY),

time: 39.8 us -> 35.3 us (0.89)
  Pallas kernels: 37.7 us -> 34.3 us
  local copies, waits for them, and re-layouts: 1.87 us -> 0.8 us
    pallas_call x1, Pallas kernels: 37.7 us -> 34.3 us  [body(): pl.pallas_call(functools.partial(kernel, norb, nsx, nsy), out_shape=pltpu...]
    unnamed x1, local copies, waits for them, and re-layouts: 1.87 us -> 0.8 us
where the time goes in v4:
time: 35.3 us; the launch traced here: 35.1 us
  Pallas kernels  34.3 us (97%)
  local copies, waits for them, and re-layouts  0.8 us (2%)
    pallas_call x1, Pallas kernels, body(): pl.pallas_call(functools.partial(kernel, norb, nsx, nsy), out_shape=pltpu...  34.3 us
    unnamed x1, local copies, waits for them, and re-layouts  0.8 us

profile of v4, /device:TPU:129, one launch (start us, length us, event | category | flops | bytes accessed | tf_op | source)
XLA Modules:
  0.0 35.1 jit_solution(14002720673935127992)
XLA Ops:
  0.0 34.3 %shard_map.46 = f32[8,8,2048]{2,1,0:T(8,128)S(1)} custom-call(s32[2,2]{1,0:T(2,128)} %owner_hbm.1, s32[2,2]{1,0:T(2,128)} %slot_hbm.1, bf16[8,8,2048]{2,1,0:T(8,128)(2,1)} %orb_hbm.1, bf16[512,512]{1,0:T(8,128)(2,1)} %constant.2.clone.mats_hbm), custom_call_target="tpu_custom_call" | custom-call | tf_op jit(solution)/shard_map/pallas_call | solution.py:267
  34.3 0.8 %copy.6 = f32[8,8,2048]{2,1,0:T(8,128)} copy(f32[8,8,2048]{2,1,0:T(8,128)S(1)} %shard_map.46) | data formatting | bytes 1048576
